TPU v7x, 32 devices: a whole 2x2x4 slice. The times are simulated.
32 devices in a mesh: ka: 8 (over z, y), row: 4 (over x, core).
Axes of the slice: x: 2, y: 2, z: 4, core: 2. Of those that a mesh axis runs over, the one named last changes fastest.
Arguments:
- packet: float32 [16, 384, 128, 128], P('ka', None, 'row'), may hold values from -6 to 6
- previous: float32 [16, 384, 128, 128], P('ka', None, 'row'), may hold values from -6 to 6
- basis_sizes: int32 [16], P('ka'), may hold values from 96 to 384, as said below
- centrifugal: float32 [16, 384], P('ka'), may hold values from 0.1 to 2
- coriolis: float32 [16, 384], replicated, may hold values from -3 to 3
- inertia: float32 [128, 128], replicated, may hold values from 0.25 to 4
- damping: float32 [128], P('row'), may hold values from 0.6 to 1
- radial_kin: float32 [128, 128], replicated, may hold values from -0.5 to 0.5
- stretch_kin: float32 [128, 128], replicated, may hold values from -0.5 to 0.5
- legendre: float32 [16, 512, 384], P('ka'), may hold values from -0.3125 to 0.3125
- potential: float32 [512, 128, 128], P(None, 'row'), may hold values from -1 to 1
Outputs:
- advanced: float32 [16, 384, 128, 128], P('ka', None, 'row')
Inputs may be any that keep to these rules, and one draw needn't show every extreme that they name: `basis_sizes`: one helicity block has exactly 384 live basis functions and another exactly 96.
All inputs are finite; a program needn't handle non-finite values.
Results may differ from a plain program's by a relative error of at most 0.0003.
Values sent between devices are 32-bit elements; how exact they have to be, the bound alone decides.
A program may use at most 192 MiB of HBM per device.

v0:
```python
import jax
import jax.numpy as jnp
from jax import lax
from jax.sharding import PartitionSpec as P


def from_behind(x, axis, by):
    peers = lax.axis_size(axis)
    pairs = [(i, i + by) for i in range(peers) if 0 <= i + by < peers]
    return lax.ppermute(x, axis, pairs)


def radial_apply(regrouped, radial_kin, stretch_kin):
    precise = lax.Precision.HIGHEST
    along_r = jnp.einsum("rs,kjsx->kjrx", radial_kin, regrouped, precision=precise)
    along_bonds = jnp.einsum("kjrz,xz->kjrx", regrouped, stretch_kin, precision=precise)
    return along_r + along_bonds


def shards(
    packet,
    previous,
    basis_sizes,
    centrifugal,
    coriolis,
    inertia,
    damping,
    radial_kin,
    stretch_kin,
    legendre,
    potential,
):
    precise = lax.Precision.HIGHEST
    blocks, basis_len, radial_local, stretch_width = packet.shape
    ka_index = lax.axis_index("ka")
    row_index = lax.axis_index("row")
    basis_index = lax.broadcasted_iota(jnp.int32, (blocks, basis_len), 1)
    live_mask = (basis_index < basis_sizes[:, None]).astype(jnp.float32)
    masked = packet * live_mask[:, :, None, None]
    inertia_local = lax.dynamic_slice_in_dim(inertia, row_index * radial_local, radial_local, 0)
    flattened = masked.reshape(blocks, basis_len, radial_local * stretch_width)
    on_grid = (
        jnp.einsum("kgj,kjy->kgy", legendre, flattened, precision=precise)
        * potential.reshape(potential.shape[0], radial_local * stretch_width)[None]
    )
    potential_term = jnp.einsum("kgj,kgy->kjy", legendre, on_grid, precision=precise).reshape(
        masked.shape
    )
    rotation_term = centrifugal[:, :, None, None] * inertia_local[None, None] * masked
    coupling_local = lax.dynamic_slice_in_dim(coriolis, ka_index * blocks, blocks, 0)
    lower_term = coupling_local[-1:, :, None, None] * masked[-1:]
    upper_block = from_behind(masked[:1], "ka", -1)
    lower_block = from_behind(lower_term, "ka", 1)
    shifted_up = jnp.concatenate([masked[1:], upper_block], 0)
    shifted_down = jnp.concatenate(
        [lower_block, coupling_local[:-1, :, None, None] * masked[:-1]], 0
    )
    coupling_term = inertia_local[None, None] * (
        coupling_local[:, :, None, None] * shifted_up + shifted_down
    )
    regrouped = lax.all_to_all(masked, "row", split_axis=1, concat_axis=2, tiled=True)
    radial_term = radial_apply(regrouped, radial_kin, stretch_kin)
    returned = lax.all_to_all(radial_term, "row", split_axis=2, concat_axis=1, tiled=True)
    hamilton = returned + rotation_term + potential_term + coupling_term
    factor = damping[None, None, :, None]
    return live_mask[:, :, None, None] * factor * (2.0 * hamilton - factor * previous)


def solution(mesh):
    in_specs = (
        P("ka", None, "row", None),
        P("ka", None, "row", None),
        P("ka"),
        P("ka", None),
        P(),
        P(),
        P("row"),
        P(),
        P(),
        P("ka", None, None),
        P(None, "row", None),
    )
    out_specs = P("ka", None, "row", None)
    return jax.shard_map(shards, mesh=mesh, in_specs=in_specs, out_specs=out_specs, check_vma=False)
```

profile of v0, /device:TPU:27, one launch (start us, length us, event | category | flops | bytes accessed | tf_op | source)
XLA Modules:
  0.0 561.2 jit_solution(8665472294457353689)
XLA Ops:
  0.0 0.0 copy-start
  0.0 0.8 compare_convert_fusion
  0.8 10.2 %broadcast_multiply_fusion = f32[2,384,32,128]{3,2,1,0:T(8,128)} fusion(f32[2,384,32,128]{3,2,1,0:T(8,128)} %param.11, f32[2,384]{1,0:T(2,128)S(1)} %compare_convert_fusion), kind=kLoop, calls=%fused_computation.11 | loop fusion | flops 3145728 | bytes 25168896 | tf_op jit(solution)/shard_map/mul | solution.py:39
  11.0 11.4 %copy.31 = f32[2,384,32,128]{3,2,0,1:T(8,128)} copy(f32[2,384,32,128]{3,2,1,0:T(8,128)} %broadcast_multiply_fusion) | data formatting | bytes 25165824 | tf_op jit(solution)/shard_map/mul | solution.py:39
  22.4 146.3 %all_to_all.36 = f32[2,384,32,128]{3,2,0,1:T(8,128)} all-to-all(f32[2,384,32,128]{3,2,0,1:T(8,128)} %copy.31), channel_id=1, replica_groups=mesh['ka'=8,'row'=4] {'row'}, dimensions={1} | all-to-all | bytes 25165824 | tf_op jit(solution)/shard_map/all_to_all | solution.py:61
  168.7 11.4 %copy.33 = f32[2,96,4,32,128]{4,3,2,1,0:T(8,128)} copy(f32[2,96,4,32,128]{4,3,0,1,2:T(8,128)} %bitcast.41) | data formatting | bytes 25165824 | tf_op jit(solution)/shard_map/all_to_all | solution.py:61
  180.1 0.0 copy-done.1
  180.1 23.9 %fusion.9 = f32[2,96,128,128]{3,2,1,0:T(8,128)} fusion(f32[2,96,128,128]{3,2,1,0:T(8,128)} %bitcast.36, f32[128,128]{1,0:T(8,128)S(1)} %copy-done.1), kind=kOutput, calls=%fused_computation.16 | convolution fusion | flops 4831838208 | bytes 25231360 | tf_op jit(solution)/shard_map/rs,kjsx->kjrx/dot_general | solution.py:15
  204.0 0.0 copy-done.2
  204.0 19.1 %bitcast_add_fusion = f32[2,96,128,128]{2,3,1,0:T(8,128)} fusion(f32[2,96,128,128]{3,2,1,0:T(8,128)} %fusion.9, f32[2,96,128,128]{3,2,1,0:T(8,128)} %bitcast.37, f32[128,128]{1,0:T(8,128)S(1)} %copy-done.2), kind=kOutput, calls=%fused_computation.9 | convolution fusion | flops 4834983936 | bytes 37814272 | tf_op jit(solution)/shard_map/kjrz,xz->kjrx/dot_general | solution.py:16
  223.1 12.7 %copy.36 = f32[2,96,128,128]{3,1,0,2:T(8,128)} copy(f32[2,96,128,128]{2,3,1,0:T(8,128)} %bitcast_add_fusion) | data formatting | bytes 25165824 | tf_op jit(solution)/shard_map/add | solution.py:17
  235.8 8.1 %all-to-all-start.1 = ((f32[2,96,128,128]{3,1,0,2:T(8,128)}), f32[2,96,128,128]{3,1,0,2:T(8,128)}, u32[]{:S(2)}, u32[]{:S(2)}) async-start(f32[2,96,128,128]{3,1,0,2:T(8,128)} %copy.36), calls=%async_computation.1 | async-start | bytes 25165824 | tf_op jit(solution)/shard_map/all_to_all | solution.py:63
  243.9 0.8 dynamic-slice_reduce_fusion.1
  244.7 12.1 %broadcast_multiply_fusion.2 = (f32[1,384,32,128]{3,2,1,0:T(8,128)}, f32[1,384,32,128]{3,2,1,0:T(8,128)}, f32[1,384,32,128]{3,2,1,0:T(8,128)}, f32[1,384,32,128]{3,2,1,0:T(8,128)}) fusion(f32[384]{0:T(512)S(1)} %get-tuple-element.5, f32[2,384,32,128]{3,2,1,0:T(8,128)} %broadcast_multiply_fusion, f32[384]{0:T(512)S(1)} %get-tuple-element.6), kind=kLoop, calls=%fused_computation.13 | loop fusion | flops 3145728 | bytes 37751808 | tf_op jit(solution)/shard_map/mul | solution.py:51
  256.8 3.1 collective-permute-start.1
  260.0 3.0 collective-permute-start
  263.0 12.9 %copy.49 = f32[2,384,32,128]{1,3,2,0:T(8,128)} copy(f32[2,384,32,128]{3,2,1,0:T(8,128)} %broadcast_multiply_fusion) | data formatting | bytes 25165824 | tf_op jit(solution)/shard_map/reshape | solution.py:41
  275.9 9.9 %copy.50 = f32[512,32,128]{0,2,1:T(8,128)} copy(f32[512,32,128]{2,1,0:T(8,128)} %param.21) | data formatting | bytes 16777216 | tf_op jit(solution)/shard_map/mul | solution.py:43
  285.8 0.0 copy-done
  285.8 30.2 %fusion.11 = f32[2,4096,512]{2,1,0:T(8,128)S(1)} fusion(f32[2,384,4096]{1,2,0:T(8,128)} %bitcast.39, f32[2,512,384]{2,1,0:T(8,128)S(1)} %copy-done), kind=kOutput, calls=%fused_computation.23 | convolution fusion | flops 19327352832 | bytes 30932992 | tf_op jit(solution)/shard_map/kgj,kjy->kgy/dot_general | solution.py:43
  316.1 0.0 slice-done
  316.1 29.4 %fusion = f32[2,4096,384]{2,1,0:T(8,128)} fusion(f32[2,512,384]{2,1,0:T(8,128)S(1)} %copy-done, f32[2,4096,512]{2,1,0:T(8,128)S(1)} %fusion.11, f32[512,4096]{0,1:T(8,128)S(1)} %bitcast.35), kind=kOutput, calls=%fused_computation.1 | convolution fusion | flops 19331547136 | bytes 39321600 | tf_op jit(solution)/shard_map/kgj,kgy->kjy/dot_general | solution.py:46
  345.5 13.0 %copy.41 = f32[2,384,32,128]{3,2,1,0:T(8,128)} copy(f32[2,384,32,128]{1,3,2,0:T(8,128)} %bitcast.38) | data formatting | bytes 25165824 | tf_op jit(solution)/shard_map/reshape | solution.py:46
  358.5 0.7 constant_dynamic-slice_fusion
  359.2 0.7 constant_dynamic-slice_fusion.1
  359.9 0.2 broadcast_multiply_fusion.3
  360.1 20.1 %all-to-all-done.1 = f32[2,96,128,128]{3,1,0,2:T(8,128)} async-done(((f32[2,96,128,128]{3,1,0,2:T(8,128)}), f32[2,96,128,128]{3,1,0,2:T(8,128)}, u32[]{:S(2)}, u32[]{:S(2)}) %all-to-all-start.1) | async-done | bytes 12582944 | tf_op jit(solution)/shard_map/all_to_all | solution.py:63
  380.2 16.5 %copy.38 = f32[2,4,96,32,128]{4,3,2,1,0:T(8,128)} copy(f32[2,4,96,32,128]{4,2,0,3,1:T(8,128)} %bitcast.11) | data formatting | bytes 25165824 | tf_op jit(solution)/shard_map/all_to_all | solution.py:63
  396.6 0.0 collective-permute-done.1
  396.7 135.5 %collective-permute-done = f32[1,384,32,128]{3,2,1,0:T(8,128)} collective-permute-done((f32[1,384,32,128]{3,2,1,0:T(8,128)}, f32[1,384,32,128]{3,2,1,0:T(8,128)}, u32[]{:S(2)}, u32[]{:S(2)}) %collective-permute-start) | collective-permute-done | bytes 6291488 | tf_op jit(solution)/shard_map/ppermute | solution.py:10
  532.2 0.0 copy-done.3
  532.2 28.7 %fusion.6 = f32[2,384,32,128]{3,2,1,0:T(8,128)} fusion(f32[1,384,32,128]{3,2,1,0:T(8,128)} %collective-permute-done, f32[1,384,32,128]{3,2,1,0:T(8,128)} %get-tuple-element.10, f32[1,384,32,128]{3,2,1,0:T(8,128)} %get-tuple-element.8, f32[1,384,32,128]{3,2,1,0:T(8,128)} %collective-permute-done.1, f32[2,384,32,128]{3,2,1,0:T(8,128)} %param.12, ...), kind=kLoop, calls=%fused_computation.8 | loop fusion | flops 47185920 | bytes 88204416 | tf_op jit(solution)/shard_map/mul | solution.py:66
  (9 shorter events, 0.0 us)
Async XLA Ops:
  0.0 285.8 %copy-start = (f32[2,512,384]{2,1,0:T(8,128)S(1)}, f32[2,512,384]{2,1,0:T(8,128)}, u32[]{:S(2)}) copy-start(f32[2,512,384]{2,1,0:T(8,128)} %param.20) | copy-start | bytes 4718596
  168.7 11.4 %copy-start.1 = (f32[128,128]{1,0:T(8,128)S(1)}, f32[128,128]{1,0:T(8,128)}, u32[]{:S(2)}) copy-start(f32[128,128]{1,0:T(8,128)} %param.18) | copy-start | bytes 196612
  180.1 23.9 %copy-start.2 = (f32[128,128]{1,0:T(8,128)S(1)}, f32[128,128]{1,0:T(8,128)}, u32[]{:S(2)}) copy-start(f32[128,128]{1,0:T(8,128)} %param.19) | copy-start | bytes 196612
  235.8 144.4 %all-to-all-start.1 = ((f32[2,96,128,128]{3,1,0,2:T(8,128)}), f32[2,96,128,128]{3,1,0,2:T(8,128)}, u32[]{:S(2)}, u32[]{:S(2)}) async-start(f32[2,96,128,128]{3,1,0,2:T(8,128)} %copy.36), calls=%async_computation.1 | async-start | bytes 25165824 | tf_op jit(solution)/shard_map/all_to_all | solution.py:63
  256.8 139.8 %collective-permute-start.1 = (f32[1,384,32,128]{3,2,1,0:T(8,128)}, f32[1,384,32,128]{3,2,1,0:T(8,128)}, u32[]{:S(2)}, u32[]{:S(2)}) collective-permute-start(f32[1,384,32,128]{3,2,1,0:T(8,128)} %get-tuple-element.7), channel_id=1, source_target_pairs={{0,4},{4,8},{8,12},{12,16},{16,20},{20,24},{24,28},{1,5},{5,9},{9,... | collective-permute-start | bytes 18874376 | tf_op jit(solution)/shard_map/ppermute | solution.py:10
  260.0 272.2 %collective-permute-start = (f32[1,384,32,128]{3,2,1,0:T(8,128)}, f32[1,384,32,128]{3,2,1,0:T(8,128)}, u32[]{:S(2)}, u32[]{:S(2)}) collective-permute-start(f32[1,384,32,128]{3,2,1,0:T(8,128)} %get-tuple-element.9), channel_id=1, source_target_pairs={{4,0},{8,4},{12,8},{16,12},{20,16},{24,20},{28,24},{5,1},{9,5},{13... | collective-permute-start | bytes 18874376 | tf_op jit(solution)/shard_map/ppermute | solution.py:10
  285.8 30.2 %slice-start = ((s8[8388608]{0:T(1024)(128)(4,1)}), s8[4194304]{0:T(1024)(128)(4,1)S(1)}, s32[]{:S(2)}) async-start(s8[8388608]{0:T(1024)(128)(4,1)} %bitcast.33), calls=%async_computation.2 | async-start | bytes 8388608
  285.8 30.2 %slice-start.1 = ((s8[8388608]{0:T(1024)(128)(4,1)}), s8[4194304]{0:T(1024)(128)(4,1)S(1)}, s32[]{:S(2)}) async-start(s8[8388608]{0:T(1024)(128)(4,1)} %bitcast.33), calls=%async_computation.3 | async-start | bytes 8388608
  345.5 14.5 %copy-start.4 = (f32[32]{0:T(128)S(1)}, f32[32]{0:T(128)}, u32[]{:S(2)}) copy-start(f32[32]{0:T(128)} %param.17) | copy-start | bytes 388
  380.2 152.0 %copy-start.3 = (f32[2,384]{1,0:T(2,128)S(1)}, f32[2,384]{1,0:T(2,128)}, u32[]{:S(2)}) copy-start(f32[2,384]{1,0:T(2,128)} %param.14) | copy-start | bytes 9220
where the time goes:
time: 569 us; the launch traced here: 561 us
  waiting for transfers between devices  156 us (27%)
  blocking collectives  146 us (26%)
  matrix products  103 us (18%)
  local copies, waits for them, and re-layouts  90 us (16%)
  other arithmetic  52 us (9%)
  starting transfers between devices  14.3 us (3%)
    all_to_all x1, blocking collectives, shards(): lax.all_to_all(masked, 'row', split_axis=1, concat_axis=2, tiled=True)  146 us
    ppermute x2, waiting for transfers between devices, from_behind(): return lax.ppermute(x, axis, pairs)  136 us
    dot_general x1, matrix products, shards(): jnp.einsum('kgj,kjy->kgy', legendre, flattened, precision=precise)  30.2 us
    dot_general x1, matrix products, shards(): jnp.einsum('kgj,kgy->kjy', legendre, on_grid, precision=precise)  29.4 us
    mul x2, other arithmetic, shards(): live_mask[:, :, None, None] * factor * (2.0 * hamilton - factor * previous)  28.9 us
    dot_general x1, matrix products, radial_apply(): jnp.einsum('rs,kjsx->kjrx', radial_kin, regrouped, precision=precise)  23.9 us
    all_to_all x1, waiting for transfers between devices, shards(): lax.all_to_all(radial_term, 'row', split_axis=2, concat_axis=1, tiled=True)  20.1 us
    dot_general x1, matrix products, radial_apply(): jnp.einsum('kjrz,xz->kjrx', regrouped, stretch_kin, precision=precise)  19.1 us
  transfers between devices with their start and end apart: 3, of which 2 were waited for; matrix products, arithmetic and copies ran while one was open for 23% of the time, Pallas kernels for 0%

commit v1 on v0

v1 whole, which is shorter than its diff:
```python
import functools

import jax
import jax.numpy as jnp
from jax import lax
from jax.experimental import pallas as pl
from jax.experimental.pallas import tpu as pltpu
from jax.sharding import PartitionSpec as P


HALVES = 2


def from_behind(x, axis, by):
    peers = lax.axis_size(axis)
    pairs = [(i, i + by) for i in range(peers) if 0 <= i + by < peers]
    return lax.ppermute(x, axis, pairs)


def rotate(x, by):
    peers = lax.axis_size("row")
    return lax.ppermute(x, "row", [(i, (i + by) % peers) for i in range(peers)])


def swap_cores(x):
    peers = lax.axis_size("row")
    return lax.ppermute(x, "row", [(i, i ^ 1) for i in range(peers)])


def split_bf16(x):
    high = x.astype(jnp.bfloat16)
    return high, (x - high.astype(jnp.float32)).astype(jnp.bfloat16)


def finish_kernel(block, base, sources, remotes, *refs):
    kin_ref, live_ref = refs[0], refs[1]
    factor_ref, turn_ref = refs[2], refs[3]
    source_refs = refs[4 : 4 + sources]
    remote_refs = refs[4 + sources : 4 + sources + 2 * remotes]
    acc_ref, out_ref = refs[-2], refs[-1]
    tile = out_ref.shape[1]
    rows = out_ref.shape[2]
    width = out_ref.shape[3]
    first = base + pl.program_id(0) * tile
    stacked = jnp.concatenate(
        [jnp.concatenate([ref[0, j] for j in range(tile)], axis=1) for ref in source_refs], axis=0
    )
    high, low = split_bf16(stacked)
    both = jnp.dot(kin_ref[...], high, preferred_element_type=jnp.float32)
    rest = jnp.dot(kin_ref[:rows, :], low, preferred_element_type=jnp.float32)
    radial = both[:rows] + both[rows:] + rest
    factor = factor_ref[...]
    turn = turn_ref[...]
    for j in range(tile):
        term = factor * radial[:, j * width : (j + 1) * width]
        for n in range(remotes):
            values, weights = remote_refs[2 * n], remote_refs[2 * n + 1]
            term = term + turn * (weights[block, first + j] * values[0, j])
        out_ref[0, j] = acc_ref[0, j] + live_ref[block, first + j] * term


def finish(acc, block, base, count, kin, live, factor, turn, sources, remotes):
    _, basis_len, rows, width = acc.shape
    tile = next(t for t in (32, 24, 16, 8, 4, 2, 1) if count % t == 0 and base % t == 0)
    whole = lambda i: (block, base // tile + i, 0, 0)
    part = lambda i: (0, i, 0, 0)
    shape = (1, tile, rows, width)
    vmem = lambda x: pl.BlockSpec(x.shape, lambda i: (0,) * x.ndim)
    smem = pl.BlockSpec(memory_space=pltpu.SMEM)
    operands = [kin, live, factor, turn]
    specs = [vmem(kin), smem, vmem(factor), vmem(turn)]
    for x in sources:
        operands.append(x)
        specs.append(pl.BlockSpec(shape, whole if x.shape[1] == basis_len else part))
    for x, weights in remotes:
        operands += [x, weights]
        specs += [pl.BlockSpec(shape, part), smem]
    operands.append(acc)
    specs.append(pl.BlockSpec(shape, whole))
    size = count * rows * width
    return pl.pallas_call(
        functools.partial(finish_kernel, block, base, len(sources), len(remotes)),
        out_shape=jax.ShapeDtypeStruct(acc.shape, acc.dtype),
        grid=(count // tile,),
        in_specs=specs,
        out_specs=pl.BlockSpec(shape, whole),
        input_output_aliases={len(operands) - 1: 0},
        cost_estimate=pl.CostEstimate(
            flops=6 * size * rows * len(sources),
            bytes_accessed=4 * size * (2 + len(sources) + len(remotes)),
            transcendentals=0,
        ),
        compiler_params=pltpu.CompilerParams(vmem_limit_bytes=40 << 20),
        name="finish",
    )(*operands)


def shards(
    packet,
    previous,
    basis_sizes,
    centrifugal,
    coriolis,
    inertia,
    damping,
    radial_kin,
    stretch_kin,
    legendre,
    potential,
):
    precise = lax.Precision.HIGH
    blocks, basis_len, rows, width = packet.shape
    peers = lax.axis_size("row")
    ka_index = lax.axis_index("ka")
    row_index = lax.axis_index("row")
    basis_index = lax.broadcasted_iota(jnp.int32, (blocks, basis_len), 1)
    live = (basis_index < basis_sizes[:, None]).astype(jnp.float32)
    coupling = lax.dynamic_slice_in_dim(coriolis, ka_index * blocks, blocks, 0)
    ones = jnp.ones_like(live)

    count = basis_len // HALVES
    order = [(b, h * count) for h in range(HALVES) for b in range(blocks)]
    piece = lambda x, b, at: x[b : b + 1, at : at + count]
    scaled = lambda x, w, b, at: piece(x, b, at) * piece(w, b, at)[:, :, None, None]

    crossed, uppers, lowers = {}, {}, {}
    for b, at in order:
        mine = scaled(packet, live, b, at)
        crossed[b, at] = [rotate(mine, 2 * d) for d in range(1, peers // 2)]
        if b == 0:
            uppers[at] = from_behind(mine, "ka", -1)
        if b == blocks - 1:
            weighted = scaled(packet, live * coupling, b, at)
            lowers[at] = from_behind(weighted, "ka", 1)
    masked = packet * live[:, :, None, None]
    partner = swap_cores(masked)

    inertia_local = lax.dynamic_slice_in_dim(inertia, row_index * rows, rows, 0)
    flattened = masked.reshape(blocks, basis_len, rows * width)
    on_grid = jnp.einsum("kgj,kjy->kgy", legendre, flattened, precision=precise)
    on_grid = (
        on_grid
        * potential.reshape(potential.shape[0], rows * width)[None]
    )
    potential_term = jnp.einsum("kgj,kgy->kjy", legendre, on_grid, precision=precise).reshape(
        masked.shape
    )
    along_bonds = jnp.einsum("kjrz,xz->kjrx", masked, stretch_kin, precision=precise)
    inside = []
    for b in range(blocks):
        term = centrifugal[b][:, None, None] * masked[b]
        if b + 1 < blocks:
            term = term + coupling[b][:, None, None] * masked[b + 1]
        if b > 0:
            term = term + coupling[b - 1][:, None, None] * masked[b - 1]
        inside.append(term)
    inside = inertia_local[None, None] * jnp.stack(inside)
    hamilton = potential_term + along_bonds + inside
    factor = damping[None, None, :, None]
    acc = live[:, :, None, None] * factor * (2.0 * hamilton - factor * previous)

    kin = lax.dynamic_slice_in_dim(radial_kin, row_index * rows, rows, 0)
    origins = [row_index, row_index ^ 1]
    for d in range(1, peers // 2):
        origin = (row_index - 2 * d) % peers
        origins += [origin, origin ^ 1]
    kin = jnp.concatenate(
        [lax.dynamic_slice_in_dim(kin, origin * rows, rows, 1) for origin in origins], 1
    )
    rounded = lax.reduce_precision(kin, 8, 7)
    kin = jnp.concatenate([rounded, kin - rounded], 0).astype(jnp.bfloat16)
    doubled = jnp.broadcast_to(2.0 * damping[:, None], (rows, width))
    turn = doubled * inertia_local
    for b, at in order:
        arrived, acc = lax.optimization_barrier((crossed[b, at], acc))
        sources = [masked, partner]
        for x in arrived:
            sources += [x, swap_cores(x)]
        remotes = []
        if b == 0:
            remotes.append((lowers[at], ones))
        if b == blocks - 1:
            remotes.append((uppers[at], coupling))
        acc = finish(acc, b, at, count, kin, live, doubled, turn, sources, remotes)
    return acc


def solution(mesh):
    in_specs = (
        P("ka", None, "row", None),
        P("ka", None, "row", None),
        P("ka"),
        P("ka", None),
        P(),
        P(),
        P("row"),
        P(),
        P(),
        P("ka", None, None),
        P(None, "row", None),
    )
    out_specs = P("ka", None, "row", None)

    return jax.shard_map(
        shards, mesh=mesh, in_specs=in_specs, out_specs=out_specs, check_vma=False
    )
```

time: 569 us -> 375 us (0.66)
  blocking collectives: 146 us -> 0 us
  local copies, waits for them, and re-layouts: 90 us -> 37.6 us
  matrix products: 103 us -> 67.9 us
  Pallas kernels: 0 us -> 34.9 us
  waiting for transfers between devices: 156 us -> 176 us
  other arithmetic: 52 us -> 34.7 us
    ppermute x0 -> x9, waiting for transfers between devices: none -> 174 us  [the longest x4 166 us: rotate(): return lax.ppermute(x, 'row', [(i, (i + by) % peers) for i in range(peers)])]
    all_to_all x1 -> x0, blocking collectives: 146 us -> none  [shards(): lax.all_to_all(masked, 'row', split_axis=1, concat_axis=2, tiled=True)]
    ppermute x2 -> x4, waiting for transfers between devices: 136 us -> 1.96 us  [from_behind(): return lax.ppermute(x, axis, pairs)]
    pallas_call x0 -> x4, Pallas kernels: none -> 34.9 us  [finish(): pl.pallas_call(functools.partial(finish_kernel, block, base, len(sources)...]
    mul x4 -> x6, other arithmetic: 51.2 us -> 23 us  [the longest x1 11.1 us: shards(): piece(x, b, at) * piece(w, b, at)[:, :, None, None]]
    all_to_all x2 -> x0, local copies, waits for them, and re-layouts: 27.8 us -> none  [the longest x1 16.5 us: shards(): lax.all_to_all(radial_term, 'row', split_axis=2, concat_axis=1, tiled=True)]
    dot_general x3 -> x2, matrix products: 73.2 us -> 49.2 us  [the longest x1 26.1 us: shards(): on_grid = jnp.einsum('kgj,kjy->kgy', legendre, flattened, precision=precise)]
    all_to_all x1 -> x0, waiting for transfers between devices: 20.1 us -> none  [shards(): lax.all_to_all(radial_term, 'row', split_axis=2, concat_axis=1, tiled=True)]
  transfers between devices with their start and end apart: 3 -> 13, of which waited for: 2 -> 8; matrix products, arithmetic and copies ran while one was open for 23% -> 35% of each run, Pallas kernels for 0% -> 7%
where the time goes in v1:
time: 375 us; the launch traced here: 370 us
  waiting for transfers between devices  176 us (47%)
  matrix products  67.9 us (18%)
  local copies, waits for them, and re-layouts  37.6 us (10%)
  Pallas kernels  34.9 us (9%)
  other arithmetic  34.7 us (9%)
  starting transfers between devices  18.8 us (5%)
    ppermute x4, waiting for transfers between devices, rotate(): return lax.ppermute(x, 'row', [(i, (i + by) % peers) for i in range(peers)])  166 us
    pallas_call x4, Pallas kernels, finish(): pl.pallas_call(functools.partial(finish_kernel, block, base, len(sources)...  34.9 us
    dot_general x1, matrix products, shards(): on_grid = jnp.einsum('kgj,kjy->kgy', legendre, flattened, precision=precise)  26.1 us
    dot_general x1, matrix products, shards(): jnp.einsum('kjrz,xz->kjrx', masked, stretch_kin, precision=precise)  23.1 us
    dot_general x1, matrix products, shards(): jnp.einsum('kgj,kgy->kjy', legendre, on_grid, precision=precise)  18.7 us
    reshape x1, local copies, waits for them, and re-layouts, shards(): flattened = masked.reshape(blocks, basis_len, rows * width)  13.8 us
    reshape x1, local copies, waits for them, and re-layouts, shards(): jnp.einsum('kgj,kgy->kjy', legendre, on_grid, precision=precise)  12.7 us
    mul x1, other arithmetic, shards(): piece(x, b, at) * piece(w, b, at)[:, :, None, None]  11.1 us
  transfers between devices with their start and end apart: 13, of which 8 were waited for; matrix products, arithmetic and copies ran while one was open for 35% of the time, Pallas kernels for 7%

profile of v1, /device:TPU:27, one launch (start us, length us, event | category | flops | bytes accessed | tf_op | source)
XLA Modules:
  0.0 370.0 jit_solution(143039232897663095)
XLA Ops:
  0.0 0.8 fusion.9.refs_1_
  0.8 10.2 %broadcast_multiply_fusion.refs_4_ = f32[2,384,32,128]{3,2,1,0:T(8,128)} fusion(f32[2,384,32,128]{3,2,1,0:T(8,128)} %param.11, f32[2,384]{1,0:T(2,128)S(1)} %fusion.9.refs_1_), kind=kLoop, calls=%fused_computation.10 | loop fusion | flops 3145728 | bytes 25168896 | tf_op jit(solution)/shard_map/mul | solution.py:135
  12.6 11.1 %slice_multiply_fusion.4 = (f32[1,192,32,128]{3,2,1,0:T(8,128)}, f32[1,192,32,128]{3,2,1,0:T(8,128)}, f32[1,192,32,128]{3,2,1,0:T(8,128)}, f32[1,192,32,128]{3,2...) fusion(f32[2,384,32,128]{3,2,1,0:T(8,128)} %param.11, f32[192]{0:T(256)S(1)} %bitcast.26, ...), kind=kLoop, calls=%fused_computation.15 | loop fusion | flops 4718592 | bytes 31461888 | tf_op jit(solution)/shard_map/mul | solution.py:124
  24.1 3.1 collective-permute-start.6
  27.2 13.8 %reshape.48 = f32[2,384,4096]{2,1,0:T(8,128)} reshape(f32[2,384,32,128]{3,2,1,0:T(8,128)} %broadcast_multiply_fusion.refs_4_) | data formatting | bytes 25165824 | tf_op jit(solution)/shard_map/reshape | solution.py:139
  41.0 10.0 %copy.23 = f32[512,32,128]{0,2,1:T(8,128)} copy(f32[512,32,128]{2,1,0:T(8,128)} %param.21) | data formatting | bytes 16777216 | tf_op jit(solution)/shard_map/mul | solution.py:142
  51.0 26.1 %fusion.13 = f32[2,4096,512]{2,1,0:T(8,128)} fusion(f32[2,384,4096]{2,1,0:T(8,128)} %reshape.48, f32[2,512,384]{2,1,0:T(8,128)S(1)} %copy-done), kind=kOutput, calls=%fused_computation.37 | convolution fusion | flops 9663676416 | bytes 30932992 | tf_op jit(solution)/shard_map/kgj,kjy->kgy/dot_general | solution.py:140
  77.1 18.7 %fusion = f32[2,4096,384]{2,1,0:T(8,128)} fusion(f32[2,512,384]{2,1,0:T(8,128)S(1)} %copy-done, f32[2,4096,512]{2,1,0:T(8,128)} %fusion.13, f32[512,4096]{0,1:T(8,128)S(1)} %bitcast.24), kind=kOutput, calls=%fused_computation.1 | convolution fusion | flops 9667870720 | bytes 39321600 | tf_op jit(solution)/shard_map/kgj,kgy->kjy/dot_general | solution.py:145
  95.8 12.7 %copy.24 = f32[2,384,32,128]{3,2,1,0:T(8,128)} copy(f32[2,384,32,128]{1,3,2,0:T(8,128)} %bitcast.25) | data formatting | bytes 25165824 | tf_op jit(solution)/shard_map/reshape | solution.py:145
  110.2 10.7 %multiply_add_fusion.1 = (f32[1,384,32,128]{3,2,1,0:T(8,128)}, f32[1,384,32,128]{3,2,1,0:T(8,128)}) fusion(f32[2,384,32,128]{3,2,1,0:T(8,128)} %broadcast_multiply_fusion.refs_4_, f32[384]{0:T(512)S(1)} %get-tuple-element.47, f32[384]{0:T(512)S(1)} %get-tuple-element.21, f32[384]{0:T(512)S(1)} %get-tuple-element.22), kind=kLoop, calls=%fused_computation.9 | loop fusion | flops 9437184 | bytes 25170432 | tf_op jit(solution)/shard_map/add | solution.py:153
  120.9 23.1 %fusion.4.refs_10_ = f32[2,384,32,128]{3,2,1,0:T(8,128)} fusion(f32[1,384,32,128]{3,2,1,0:T(8,128)} %get-tuple-element.30, f32[1,384,32,128]{3,2,1,0:T(8,128)} %get-tuple-element.29, f32[2,384,32,128]{3,2,1,0:T(8,128)} %param.12, f32[2,384,32,128]{3,2,1,0:T(8,128)} %copy.24, f32[32]{0:T(128)S(1)} %copy-done.6, f32[32,128]{1,0:T(8,128)S(1)} %get-tuple-element.26, ...), kind=kOutput, calls=%fused_computation.6 | convolution fusion | flops 2441084928 | bytes 63094912 | tf_op jit(solution)/shard_map/kjrz,xz->kjrx/dot_general | solution.py:148
  144.6 1.2 collective-permute-start.3
  145.8 3.0 collective-permute-start.8
  149.1 1.1 collective-permute-done.5.refs_7_
  150.3 10.2 %finish.4.refs_10_ = f32[2,384,32,128]{3,2,1,0:T(8,128)} custom-call(bf16[64,128]{1,0:T(8,128)(2,1)S(1)} %pad_maximum_fusion.1.refs_0_, f32[2,384]{1,0:T(2,128)S(1)} %fusion.9.refs_1_, f32[32,128]{1,0:T(8,128)S(1)} %broadcast_in_dim.4.refs_2_, f32[32,128]{1,0:T(8,128)S(1)} %get-tuple-element.25.refs_3_, ...), custom_call_target="tpu_custom_call", output_to_operand_aliasing={{}: (10, {})} | custom-call | flops 603979776 | bytes 22020096 | tf_op jit(solution)/shard_map/finish/pallas_call | solution.py:81
  160.5 54.0 %collective-permute-done.3.refs_6_ = f32[1,192,32,128]{3,2,1,0:T(8,128)S(1)} collective-permute-done((f32[1,192,32,128]{3,2,1,0:T(8,128)}, f32[1,192,32,128]{3,2,1,0:T(8,128)S(1)}, u32[]{:S(2)}, u32[]{:S(2)}) %collective-permute-start.3) | collective-permute-done | bytes 3145760 | tf_op jit(solution)/shard_map/ppermute | solution.py:22
  214.5 0.8 collective-permute-start.7
  215.3 1.2 collective-permute-start.2
  216.6 1.9 collective-permute-start.10
  218.5 2.1 collective-permute-done.7.refs_7_
  220.6 8.6 %finish.5.refs_10_ = f32[2,384,32,128]{3,2,1,0:T(8,128)} custom-call(bf16[64,128]{1,0:T(8,128)(2,1)S(1)} %pad_maximum_fusion.1.refs_0_, f32[2,384]{1,0:T(2,128)S(1)} %fusion.9.refs_1_, f32[32,128]{1,0:T(8,128)S(1)} %broadcast_in_dim.4.refs_2_, f32[32,128]{1,0:T(8,128)S(1)} %get-tuple-element.25.refs_3_, ...), custom_call_target="tpu_custom_call", output_to_operand_aliasing={{}: (10, {})} | custom-call | flops 603979776 | bytes 22020096 | tf_op jit(solution)/shard_map/finish/pallas_call | solution.py:81
  229.2 55.8 %collective-permute-done.2.refs_6_ = f32[1,192,32,128]{3,2,1,0:T(8,128)S(1)} collective-permute-done((f32[1,192,32,128]{3,2,1,0:T(8,128)S(1)}, f32[1,192,32,128]{3,2,1,0:T(8,128)S(1)}, u32[]{:S(2)}, u32[]{:S(2)}) %collective-permute-start.2) | collective-permute-done | bytes 3145760 | tf_op jit(solution)/shard_map/ppermute | solution.py:22
  285.0 0.9 collective-permute-start.9
  285.9 1.2 collective-permute-start.1
  287.1 3.0 collective-permute-start.12
  290.1 1.0 collective-permute-done.9.refs_7_
  291.2 8.0 %finish.6.refs_10_ = f32[2,384,32,128]{3,2,1,0:T(8,128)} custom-call(bf16[64,128]{1,0:T(8,128)(2,1)S(1)} %pad_maximum_fusion.1.refs_0_, f32[2,384]{1,0:T(2,128)S(1)} %fusion.9.refs_1_, f32[32,128]{1,0:T(8,128)S(1)} %broadcast_in_dim.4.refs_2_, f32[32,128]{1,0:T(8,128)S(1)} %get-tuple-element.25.refs_3_, ...), custom_call_target="tpu_custom_call", output_to_operand_aliasing={{}: (10, {})} | custom-call | flops 603979776 | bytes 22020096 | tf_op jit(solution)/shard_map/finish/pallas_call | solution.py:81
  299.2 56.6 %collective-permute-done.1.refs_6_ = f32[1,192,32,128]{3,2,1,0:T(8,128)S(1)} collective-permute-done((f32[1,192,32,128]{3,2,1,0:T(8,128)}, f32[1,192,32,128]{3,2,1,0:T(8,128)S(1)}, u32[]{:S(2)}, u32[]{:S(2)}) %collective-permute-start.1) | collective-permute-done | bytes 3145760 | tf_op jit(solution)/shard_map/ppermute | solution.py:22
  355.7 0.9 collective-permute-start.11
  356.6 2.0 collective-permute-done.12.refs_8_
  358.5 3.3 collective-permute-done.11.refs_7_
  361.9 8.1 %finish.7 = f32[2,384,32,128]{3,2,1,0:T(8,128)} custom-call(bf16[64,128]{1,0:T(8,128)(2,1)S(1)} %pad_maximum_fusion.1.refs_0_, f32[2,384]{1,0:T(2,128)S(1)} %fusion.9.refs_1_, f32[32,128]{1,0:T(8,128)S(1)} %broadcast_in_dim.4.refs_2_, f32[32,128]{1,0:T(8,128)S(1)} %get-tuple-element.25.refs_3_, ...), custom_call_target="tpu_custom_call", output_to_operand_aliasing={{}: (10, {})} | custom-call | flops 603979776 | bytes 22020096 | tf_op jit(solution)/shard_map/finish/pallas_call | solution.py:81
  (39 shorter events, 4.5 us)
Async XLA Ops:
  0.0 51.0 %copy-start = (f32[2,512,384]{2,1,0:T(8,128)S(1)}, f32[2,512,384]{2,1,0:T(8,128)}, u32[]{:S(2)}) copy-start(f32[2,512,384]{2,1,0:T(8,128)} %param.20) | copy-start | bytes 4718596
  0.8 10.8 %copy-start.8 = (s32[2]{0:T(128)S(1)}, s32[2]{0:T(128)}, u32[]{:S(2)}) copy-start(s32[2]{0:T(128)} %param.13) | copy-start | bytes 28
  11.0 139.2 %collective-permute-start = (f32[2,384,32,128]{3,2,1,0:T(8,128)}, f32[2,384,32,128]{3,2,1,0:T(8,128)}, u32[]{:S(2)}, u32[]{:S(2)}) collective-permute-start(f32[2,384,32,128]{3,2,1,0:T(8,128)} %broadcast_multiply_fusion.refs_4_), channel_id=1, source_target_pairs={{0,1},{1,0},{2,3},{3,2},{4,5},{5,4},{6,7},{7,6},{8,9},{9,8},{10,11... | collective-permute-start | bytes 37748744 | tf_op jit(solution)/shard_map/ppermute | solution.py:27
  23.8 120.3 %collective-permute-start.4 = (f32[1,192,32,128]{3,2,1,0:T(8,128)}, f32[1,192,32,128]{3,2,1,0:T(8,128)}, u32[]{:S(2)}, u32[]{:S(2)}) collective-permute-start(f32[1,192,32,128]{3,2,1,0:T(8,128)} %get-tuple-element.35), channel_id=1, source_target_pairs={{0,2},{1,3},{2,0},{3,1},{4,6},{5,7},{6,4},{7,5},{8,10},{9,11},{10,... | collective-permute-start | bytes 9437192 | tf_op jit(solution)/shard_map/ppermute | solution.py:22
  24.1 125.1 %collective-permute-start.6 = (f32[1,192,32,128]{3,2,1,0:T(8,128)}, f32[1,192,32,128]{3,2,1,0:T(8,128)}, u32[]{:S(2)}, u32[]{:S(2)}) collective-permute-start(f32[1,192,32,128]{3,2,1,0:T(8,128)} %get-tuple-element.32), channel_id=1, source_target_pairs={{0,4},{4,8},{8,12},{12,16},{16,20},{20,24},{24,28},{1,5},{5,9},{9,... | collective-permute-start | bytes 9437192 | tf_op jit(solution)/shard_map/ppermute | solution.py:17
  51.0 26.1 %copy-start.2 = (f32[512,32,128]{0,2,1:T(8,128)S(1)}, f32[512,32,128]{0,2,1:T(8,128)}, u32[]{:S(2)}) copy-start(f32[512,32,128]{0,2,1:T(8,128)} %copy.23) | copy-start | bytes 25165828
  77.1 18.7 %copy-start.6 = (f32[32]{0:T(128)S(1)}, f32[32]{0:T(128)}, u32[]{:S(2)}) copy-start(f32[32]{0:T(128)} %param.17) | copy-start | bytes 388
  95.8 12.7 %copy-start.7 = (f32[2,384]{1,0:T(2,128)S(1)}, f32[2,384]{1,0:T(2,128)}, u32[]{:S(2)}) copy-start(f32[2,384]{1,0:T(2,128)} %param.14) | copy-start | bytes 9220
  110.2 10.7 %copy-start.4 = (f32[128,128]{1,0:T(8,128)S(1)}, f32[128,128]{1,0:T(8,128)}, u32[]{:S(2)}) copy-start(f32[128,128]{1,0:T(8,128)} %param.19) | copy-start | bytes 196612
  120.9 28.0 %copy-start.5 = (f32[128,128]{1,0:T(8,128)S(1)}, f32[128,128]{1,0:T(8,128)}, u32[]{:S(2)}) copy-start(f32[128,128]{1,0:T(8,128)} %param.18) | copy-start | bytes 196612
  144.1 6.2 %collective-permute-start.5 = (f32[1,192,32,128]{3,2,1,0:T(8,128)}, f32[1,192,32,128]{3,2,1,0:T(8,128)}, u32[]{:S(2)}, u32[]{:S(2)}) collective-permute-start(f32[1,192,32,128]{3,2,1,0:T(8,128)} %collective-permute-done.4.refs_6_), channel_id=1, source_target_pairs={{0,1},{1,0},{2,3},{3,2},{4,5},{5,4},{6,7},{7,6},{8,9},{9,8},{10,11... | collective-permute-start | bytes 9437192 | tf_op jit(solution)/shard_map/ppermute | solution.py:27
  144.6 69.9 %collective-permute-start.3 = (f32[1,192,32,128]{3,2,1,0:T(8,128)}, f32[1,192,32,128]{3,2,1,0:T(8,128)S(1)}, u32[]{:S(2)}, u32[]{:S(2)}) collective-permute-start(f32[1,192,32,128]{3,2,1,0:T(8,128)} %get-tuple-element.36), channel_id=1, source_target_pairs={{0,2},{1,3},{2,0},{3,1},{4,6},{5,7},{6,4},{7,5},{8,10},{9,11},{10,... | collective-permute-start | bytes 9437192 | tf_op jit(solution)/shard_map/ppermute | solution.py:22
  145.8 72.6 %collective-permute-start.8 = (f32[1,192,32,128]{3,2,1,0:T(8,128)}, f32[1,192,32,128]{3,2,1,0:T(8,128)}, u32[]{:S(2)}, u32[]{:S(2)}) collective-permute-start(f32[1,192,32,128]{3,2,1,0:T(8,128)} %get-tuple-element.35), channel_id=1, source_target_pairs={{4,0},{8,4},{12,8},{16,12},{20,16},{24,20},{28,24},{5,1},{9,5},{13... | collective-permute-start | bytes 9437192 | tf_op jit(solution)/shard_map/ppermute | solution.py:17
  150.3 65.0 %copy-start.3 = (f32[1,192,32,128]{3,2,1,0:T(8,128)S(1)}, f32[1,192,32,128]{3,2,1,0:T(8,128)}, u32[]{:S(2)}) copy-start(f32[1,192,32,128]{3,2,1,0:T(8,128)} %get-tuple-element.33) | copy-start | bytes 9437188
  214.5 6.1 %collective-permute-start.7 = (f32[1,192,32,128]{3,2,1,0:T(8,128)S(1)}, f32[1,192,32,128]{3,2,1,0:T(8,128)S(1)}, u32[]{:S(2)}, u32[]{:S(2)}) collective-permute-start(f32[1,192,32,128]{3,2,1,0:T(8,128)S(1)} %collective-permute-done.3.refs_6_), channel_id=1, source_target_pairs={{0,1},{1,0},{2,3},{3,2},{4,5},{5,4},{6,7},{7,6},{8,9},{9,8},{10,11... | collective-permute-start | bytes 9437192 | tf_op jit(solution)/shard_map/ppermute | solution.py:27
  215.3 69.7 %collective-permute-start.2 = (f32[1,192,32,128]{3,2,1,0:T(8,128)S(1)}, f32[1,192,32,128]{3,2,1,0:T(8,128)S(1)}, u32[]{:S(2)}, u32[]{:S(2)}) collective-permute-start(f32[1,192,32,128]{3,2,1,0:T(8,128)S(1)} %copy-done.3), channel_id=1, source_target_pairs={{0,2},{1,3},{2,0},{3,1},{4,6},{5,7},{6,4},{7,5},{8,10},{9,11},{10,... | collective-permute-start | bytes 9437192 | tf_op jit(solution)/shard_map/ppermute | solution.py:22
  216.6 73.5 %collective-permute-start.10 = (f32[1,192,32,128]{3,2,1,0:T(8,128)}, f32[1,192,32,128]{3,2,1,0:T(8,128)S(1)}, u32[]{:S(2)}, u32[]{:S(2)}) collective-permute-start(f32[1,192,32,128]{3,2,1,0:T(8,128)} %get-tuple-element.31), channel_id=1, source_target_pairs={{0,4},{4,8},{8,12},{12,16},{16,20},{20,24},{24,28},{1,5},{5,9},{9,... | collective-permute-start | bytes 9437192 | tf_op jit(solution)/shard_map/ppermute | solution.py:17
  285.0 6.1 %collective-permute-start.9 = (f32[1,192,32,128]{3,2,1,0:T(8,128)S(1)}, f32[1,192,32,128]{3,2,1,0:T(8,128)S(1)}, u32[]{:S(2)}, u32[]{:S(2)}) collective-permute-start(f32[1,192,32,128]{3,2,1,0:T(8,128)S(1)} %collective-permute-done.2.refs_6_), channel_id=1, source_target_pairs={{0,1},{1,0},{2,3},{3,2},{4,5},{5,4},{6,7},{7,6},{8,9},{9,8},{10,11... | collective-permute-start | bytes 9437192 | tf_op jit(solution)/shard_map/ppermute | solution.py:27
  285.9 69.9 %collective-permute-start.1 = (f32[1,192,32,128]{3,2,1,0:T(8,128)}, f32[1,192,32,128]{3,2,1,0:T(8,128)S(1)}, u32[]{:S(2)}, u32[]{:S(2)}) collective-permute-start(f32[1,192,32,128]{3,2,1,0:T(8,128)} %get-tuple-element.34), channel_id=1, source_target_pairs={{0,2},{1,3},{2,0},{3,1},{4,6},{5,7},{6,4},{7,5},{8,10},{9,11},{10,... | collective-permute-start | bytes 9437192 | tf_op jit(solution)/shard_map/ppermute | solution.py:22
  287.1 71.5 %collective-permute-start.12 = (f32[1,192,32,128]{3,2,1,0:T(8,128)}, f32[1,192,32,128]{3,2,1,0:T(8,128)S(1)}, u32[]{:S(2)}, u32[]{:S(2)}) collective-permute-start(f32[1,192,32,128]{3,2,1,0:T(8,128)} %get-tuple-element.33), channel_id=1, source_target_pairs={{4,0},{8,4},{12,8},{16,12},{20,16},{24,20},{28,24},{5,1},{9,5},{13... | collective-permute-start | bytes 9437192 | tf_op jit(solution)/shard_map/ppermute | solution.py:17
  355.7 6.1 %collective-permute-start.11 = (f32[1,192,32,128]{3,2,1,0:T(8,128)S(1)}, f32[1,192,32,128]{3,2,1,0:T(8,128)S(1)}, u32[]{:S(2)}, u32[]{:S(2)}) collective-permute-start(f32[1,192,32,128]{3,2,1,0:T(8,128)S(1)} %collective-permute-done.1.refs_6_), channel_id=1, source_target_pairs={{0,1},{1,0},{2,3},{3,2},{4,5},{5,4},{6,7},{7,6},{8,9},{9,8},{10,11... | collective-permute-start | bytes 9437192 | tf_op jit(solution)/shard_map/ppermute | solution.py:27
  361.9 8.1 %copy-start.1 = (f32[2,512,384]{2,1,0:T(8,128)S(1)}, f32[2,512,384]{2,1,0:T(8,128)}, u32[]{:S(2)}) copy-start(f32[2,512,384]{2,1,0:T(8,128)} %param.20) | copy-start | bytes 4718596
